TPU v7x, 32 devices: a whole 2x2x4 slice. The times are simulated.
32 devices in a mesh: grp: 2 (over y), occ: 4 (over z), aux: 2 (over x), vir: 2 (over core).
Axes of the slice: x: 2, y: 2, z: 4, core: 2. Of those that a mesh axis runs over, the one named last changes fastest.
Arguments:
- integrals: bfloat16 [4, 1024, 8, 1280], P('occ', 'aux', 'grp', 'vir'), parts along dimension 2, may hold values from -0.59765625 to 0.59765625
- occ_energy: float32 [8], P('grp'), parts along dimension 0, may hold values from -1.5 to -0.3
- vir_energy: float32 [2560], P('grp'), parts along dimension 0, may hold values from 0.2 to 3
- round_owner: int32 [4], P('grp'), parts along dimension 0, may hold values from 0 to 3, as said below
Outputs:
- gamma_field: float32 [8, 1024, 4, 1280], P('grp', 'aux', 'occ', 'vir'), parts along dimension 0
There are 2 independent parts, one for each index of `grp`. A program takes and returns all parts, laid end to end along the dimension named above; each array names one. Nothing has to cross between parts.
Inputs may be any that keep to these rules, and one draw needn't show every extreme that they name: `round_owner`: the 2 owners are distinct.
All inputs are finite; a program needn't handle non-finite values.
Results may differ from a plain program's by a relative error of at most 0.0085.
Values may be sent and summed in bfloat16 or wider, within the bound.
No kernel may reach another device: no remote copies, remote signals or barrier semaphores. Data moves between devices by JAX's collectives and lax.ppermute only.
A program may use at most 64 MiB of HBM per device.

v0:
```python
import jax
import jax.numpy as jnp
from jax import lax
from jax.sharding import PartitionSpec as P

ROUNDS = 2


def from_root(value, axis, root):
    mine = lax.axis_index(axis) == root
    return lax.psum(jnp.where(mine, value, jnp.zeros_like(value)), axis)


def local(integrals, occ_energy, vir_energy, round_owner):
    regrouped = lax.all_to_all(integrals, "occ", split_axis=2, concat_axis=0, tiled=True)
    occ_width = regrouped.shape[2]
    vir_width = regrouped.shape[3]
    energy_i = lax.dynamic_slice_in_dim(occ_energy, lax.axis_index("occ") * occ_width, occ_width)
    energy_a = lax.dynamic_slice_in_dim(vir_energy, lax.axis_index("vir") * vir_width, vir_width)
    gamma_total = jnp.zeros(regrouped.shape, jnp.float32)
    for turn_index in range(ROUNDS):
        owner = round_owner[turn_index]
        owner_half = from_root(regrouped, "occ", owner)
        owner_whole = lax.all_gather(owner_half, "vir", axis=3, tiled=True)
        energy_j = lax.dynamic_slice_in_dim(occ_energy, owner * occ_width, occ_width)
        partial_value = jnp.einsum(
            "sria,srjb->ijab", regrouped, owner_whole, preferred_element_type=jnp.float32
        )
        base = energy_i[:, None, None] + energy_j[None, :, None] - energy_a[None, None, :]
        pair_block = lax.psum(partial_value.astype(jnp.bfloat16), "aux").astype(jnp.float32)
        amplitude = (pair_block / (base[..., None] - vir_energy)).astype(jnp.bfloat16)
        gamma_total = gamma_total + jnp.einsum(
            "ijab,srjb->sria", amplitude, owner_whole, preferred_element_type=jnp.float32
        )
    return gamma_total


def solution(mesh):
    placed = (P("occ", "aux", "grp", "vir"), P("grp"), P("grp"), P("grp"))
    return jax.shard_map(
        local, mesh=mesh, in_specs=placed, out_specs=P("grp", "aux", "occ", "vir"), check_vma=False
    )
```

profile of v0, /device:TPU:0, one launch (start us, length us, event | category | flops | bytes accessed | tf_op | source)
XLA Modules:
  0.0 432.3 jit_solution(8235440638298763735)
XLA Ops:
  6.5 3.6 copy.11
  10.1 0.0 copy-start.2
  10.1 6.4 %all-to-all-start = ((bf16[1,512,4,640]{3,1,0,2:T(8,128)(2,1)}), bf16[1,512,4,640]{3,1,0,2:T(8,128)(2,1)S(1)}, u32[]{:S(2)}, u32[]{:S(2)}) async-start(bf16[1,512,4,640]{3,1,0,2:T(8,128)(2,1)} %copy.11), calls=%async_computation | async-start | bytes 5242880 | tf_op jit(solution)/shard_map/all_to_all | solution.py:15
  16.5 0.0 all-reduce.5.cloned.1.call-start
  16.5 0.0 copy-done.2
  16.6 0.7 fusion.41
  18.5 57.4 %all-to-all-done = bf16[1,512,4,640]{3,1,0,2:T(8,128)(2,1)S(1)} async-done(((bf16[1,512,4,640]{3,1,0,2:T(8,128)(2,1)}), bf16[1,512,4,640]{3,1,0,2:T(8,128)(2,1)S(1)}, u32[]{:S(2)}, u32[]{:S(2)}) %all-to-all-start) | async-done | bytes 2621472 | tf_op jit(solution)/shard_map/all_to_all | solution.py:15
  76.0 2.8 fusion.28
  78.8 0.0 all-reduce.5.cloned.1.call-update
  78.8 0.0 all-gather.3.cloned.1.call-start
  78.8 188.5 %all-reduce.5.cloned.1.call-done = (bf16[4,512,1,640]{3,1,0,2:T(8,128)(2,1)}, bf16[4,512,1,640]{3,1,0,2:T(8,128)(2,1)}) async-done(((bf16[4,512,1,640]{3,1,0,2:T(8,128)(2,1)}, bf16[4,512,1,640]{3,1,0,2:T(8,128)(2,1)}), (bf16[4,512,1,640]{3,1,0,2:T(8,128)(2,1)}, bf16[4,512,1,640]{3,1,0,2:T(8,128)(2,1)})) %all-reduce.5.cloned.1.call-update) | async-done | bytes 5242896 | tf_op jit(solution)/shard_map/psum | solution.py:11
  267.3 0.0 all-gather.3.cloned.1.call-update
  267.4 0.0 all-gather.5.cloned.1.call-start
  267.4 0.7 all-gather.5.cloned.1.call-update
  268.1 0.0 all-reduce.7.cloned.1.call-start
  268.1 14.9 %all-gather.3.cloned.1.call-done = bf16[4,512,1,1280]{3,1,0,2:T(8,128)(2,1)} async-done(((bf16[4,512,1,640]{3,1,0,2:T(8,128)(2,1)}), bf16[4,512,1,1280]{3,1,0,2:T(8,128)(2,1)}) %all-gather.3.cloned.1.call-update) | async-done | bytes 5242896 | tf_op jit(solution)/shard_map/all_gather | solution.py:24
  283.0 8.0 %fusion.20 = bf16[1,1,640,1280]{2,3,0,1:T(8,128)(2,1)} fusion(bf16[4,512,1,1280]{3,1,0,2:T(8,128)(2,1)} %all-gather.3.cloned.1.call-done, bf16[1,512,4,640]{3,1,0,2:T(8,128)(2,1)S(1)} %all-to-all-done), kind=kOutput, calls=%fused_computation.15 | convolution fusion | flops 3356262400 | bytes 9502720 | tf_op jit(solution)/shard_map/sria,srjb->ijab/dot_general | solution.py:26
  291.0 9.9 %all-gather.5.cloned.1.call-done = bf16[4,512,1,1280]{3,1,0,2:T(8,128)(2,1)} async-done(((bf16[4,512,1,640]{3,1,0,2:T(8,128)(2,1)}), bf16[4,512,1,1280]{3,1,0,2:T(8,128)(2,1)}) %all-gather.5.cloned.1.call-update) | async-done | bytes 5242896 | tf_op jit(solution)/shard_map/all_gather | solution.py:24
  300.9 8.0 %fusion.23 = bf16[1,1,640,1280]{2,3,0,1:T(8,128)(2,1)} fusion(bf16[4,512,1,1280]{3,1,0,2:T(8,128)(2,1)} %all-gather.5.cloned.1.call-done, bf16[1,512,4,640]{3,1,0,2:T(8,128)(2,1)S(1)} %all-to-all-done), kind=kOutput, calls=%fused_computation.16 | convolution fusion | flops 3356262400 | bytes 9502720 | tf_op jit(solution)/shard_map/sria,srjb->ijab/dot_general | solution.py:26
  308.8 0.0 copy-start
  308.9 0.0 copy-start.1
  308.9 0.0 all-reduce.7.cloned.1.call-update
  312.8 0.0 copy-done
  312.9 0.7 fusion.40
  316.0 0.0 copy-done.1
  316.0 0.1 dynamic-slice_subtract_fusion.1
  316.1 82.9 %all-reduce.7.cloned.1.call-done = (bf16[1,1,640,1280]{2,3,0,1:T(8,128)(2,1)}, bf16[1,1,640,1280]{2,3,0,1:T(8,128)(2,1)}) async-done(((bf16[1,1,640,1280]{2,3,0,1:T(8,128)(2,1)}, bf16[1,1,640,1280]{2,3,0,1:T(8,128)(2,1)}), (bf16[1,1,640,1280]{2,3,0,1:T(8,128)(2,1)}, bf16[1,1,640,1280]{2,3,0,1:T(8,128)(2,1)})) %all-reduce.7.cloned.1.call-update) | async-done | bytes 3276816 | tf_op jit(solution)/shard_map/psum | solution.py:30
  399.0 0.0 copy-start.3
  399.0 7.2 %fusion = f32[4,512,640]{2,1,0:T(8,128)S(1)} fusion(bf16[4,512,1,1280]{3,1,0,2:T(8,128)(2,1)} %all-gather.5.cloned.1.call-done, bf16[1,1,640,1280]{2,3,0,1:T(8,128)(2,1)} %get-tuple-element.7, f32[640]{0:T(1024)S(1)} %get-tuple-element.12, f32[1280]{0:T(1024)S(1)} %copy-done.1), kind=kOutput, calls=%fused_computation | convolution fusion | flops 3358720000 | bytes 12131840 | tf_op jit(solution)/shard_map/ijab,srjb->sria/dot_general | solution.py:32
  406.2 0.0 copy-done.3
  406.2 9.3 %add_bitcast_fusion = f32[4,512,1,640]{3,1,0,2:T(8,128)} fusion(f32[4,512,640]{2,1,0:T(8,128)S(1)} %fusion, bf16[4,512,1,1280]{3,1,0,2:T(8,128)(2,1)} %all-gather.3.cloned.1.call-done, bf16[1,1,640,1280]{2,3,0,1:T(8,128)(2,1)S(1)} %copy-done.3, f32[1280]{0:T(1024)S(1)} %copy-done.1, f32[640]{0:T(1024)S(1)} %get-tuple-element.11), kind=kOutput, calls=%fused_computation.8 | convolution fusion | flops 3360030720 | bytes 17374720 | tf_op jit(solution)/shard_map/ijab,srjb->sria/dot_general | solution.py:32
  415.5 10.2 %copy.16 = f32[4,512,1,640]{3,2,1,0:T(1,128)} copy(f32[4,512,1,640]{3,1,0,2:T(8,128)} %add_bitcast_fusion) | data formatting | bytes 10485760 | tf_op jit(solution)/shard_map/add | solution.py:32
Async XLA Ops:
  10.1 6.5 %copy-start.2 = (s32[2]{0:T(128)S(1)}, s32[2]{0:T(128)}, u32[]{:S(2)}) copy-start(s32[2]{0:T(128)} %param.7) | copy-start | bytes 28
  10.1 65.9 %all-to-all-start = ((bf16[1,512,4,640]{3,1,0,2:T(8,128)(2,1)}), bf16[1,512,4,640]{3,1,0,2:T(8,128)(2,1)S(1)}, u32[]{:S(2)}, u32[]{:S(2)}) async-start(bf16[1,512,4,640]{3,1,0,2:T(8,128)(2,1)} %copy.11), calls=%async_computation | async-start | bytes 5242880 | tf_op jit(solution)/shard_map/all_to_all | solution.py:15
  16.5 250.8 %all-reduce.5.cloned.1.call-start = ((), (), s32[]{:S(2)}) async-start(), calls=%async_computation.3 | async-start | bytes 10485760 | tf_op jit(solution)/shard_map/psum | solution.py:11
  78.8 204.2 %all-gather.3.cloned.1.call-start = ((), (), s32[]{:S(2)}) async-start(), calls=%async_computation.1 | async-start | bytes 7864320 | tf_op jit(solution)/shard_map/all_gather | solution.py:24
  267.4 33.5 %all-gather.5.cloned.1.call-start = ((), (), s32[]{:S(2)}) async-start(), calls=%async_computation.2 | async-start | bytes 7864320 | tf_op jit(solution)/shard_map/all_gather | solution.py:24
  268.1 130.9 %all-reduce.7.cloned.1.call-start = ((), (), s32[]{:S(2)}) async-start(), calls=%async_computation.4 | async-start | bytes 6553600 | tf_op jit(solution)/shard_map/psum | solution.py:30
  308.8 4.0 copy-start
  308.9 7.1 %copy-start.1 = (f32[1280]{0:T(1024)S(1)}, f32[1280]{0:T(1024)}, u32[]{:S(2)}) copy-start(f32[1280]{0:T(1024)} %param.6) | copy-start | bytes 15364
  399.0 7.2 %copy-start.3 = (bf16[1,1,640,1280]{2,3,0,1:T(8,128)(2,1)S(1)}, bf16[1,1,640,1280]{2,3,0,1:T(8,128)(2,1)}, u32[]{:S(2)}) copy-start(bf16[1,1,640,1280]{2,3,0,1:T(8,128)(2,1)} %get-tuple-element.8) | copy-start | bytes 4915204
Sparse Core Ops, SparseCore 0:
  78.9 188.3 all-reduce.4
  268.9 14.0 all-gather.2
  284.6 16.2 all-gather.4
  309.0 89.9 all-reduce.6
where the time goes:
time: 433 us; the launch traced here: 432 us
  waiting for transfers between devices  354 us (82%)
  matrix products  32.4 us (7%)
  between operations  20.9 us (5%)
  local copies, waits for them, and re-layouts  15.1 us (3%)
  starting transfers between devices  6.57 us (2%)
    psum x1, waiting for transfers between devices, from_root(): return lax.psum(jnp.where(mine, value, jnp.zeros_like(value)), axis)  188 us
    psum x1, waiting for transfers between devices, local(): lax.psum(partial_value.astype(jnp.bfloat16), 'aux').astype(jnp.float32)  82.9 us
    all_to_all x1, waiting for transfers between devices, local(): lax.all_to_all(integrals, 'occ', split_axis=2, concat_axis=0, tiled=True)  57.4 us
    all_gather x2, waiting for transfers between devices, local(): owner_whole = lax.all_gather(owner_half, 'vir', axis=3, tiled=True)  24.8 us
    dot_general x2, matrix products, local(): jnp.einsum('ijab,srjb->sria', amplitude, owner_whole, preferred_element_t...  16.5 us
    dot_general x2, matrix products, local(): jnp.einsum('sria,srjb->ijab', regrouped, owner_whole, preferred_element_t...  15.9 us
    add x1, local copies, waits for them, and re-layouts, local(): gamma_total + jnp.einsum('ijab,srjb->sria', amplitude, owner_whole, prefe...  10.2 us
  transfers between devices with their start and end apart: 5, of which 5 were waited for; matrix products, arithmetic and copies ran while one was open for 2% of the time, Pallas kernels for 0%

commit v1 on v0

--- a/solution.py
+++ b/solution.py
@@ -12,7 +12,10 @@
 
 
 def local(integrals, occ_energy, vir_energy, round_owner):
-    regrouped = lax.all_to_all(integrals, "occ", split_axis=2, concat_axis=0, tiled=True)
+    regrouped = jnp.concatenate(
+        lax.all_to_all(jnp.stack(jnp.split(integrals, lax.axis_size("occ"), axis=2)), "occ", 0, 0),
+        axis=0,
+    )
     occ_width = regrouped.shape[2]
     vir_width = regrouped.shape[3]
     energy_i = lax.dynamic_slice_in_dim(occ_energy, lax.axis_index("occ") * occ_width, occ_width)

time: 433 us -> 445 us (1.028)
  local copies, waits for them, and re-layouts: 15.1 us -> 23.3 us
    split x0 -> x1, local copies, waits for them, and re-layouts: none -> 8.82 us  [local(): jnp.split(integrals, lax.axis_size('occ'), axis=2)]
where the time goes in v1:
time: 445 us
  waiting for transfers between devices  355 us (80%)
  matrix products  32.8 us (7%)
  local copies, waits for them, and re-layouts  23.3 us (5%)
  between operations  20.6 us (5%)
  starting transfers between devices  6.75 us (2%)
  other arithmetic  6.4 us (1%)
    psum x1, waiting for transfers between devices, from_root(): return lax.psum(jnp.where(mine, value, jnp.zeros_like(value)), axis)  188 us
    psum x1, waiting for transfers between devices, local(): lax.psum(partial_value.astype(jnp.bfloat16), 'aux').astype(jnp.float32)  83.1 us
    all_to_all x1, waiting for transfers between devices, local(): lax.all_to_all(jnp.stack(jnp.split(integrals, lax.axis_size('occ'), axis=...  57.7 us
    all_gather x2, waiting for transfers between devices, local(): owner_whole = lax.all_gather(owner_half, 'vir', axis=3, tiled=True)  24.9 us
    dot_general x2, matrix products, local(): jnp.einsum('ijab,srjb->sria', amplitude, owner_whole, preferred_element_t...  17.1 us
    dot_general x2, matrix products, local(): jnp.einsum('sria,srjb->ijab', regrouped, owner_whole, preferred_element_t...  15.8 us
    add x1, local copies, waits for them, and re-layouts, local(): gamma_total + jnp.einsum('ijab,srjb->sria', amplitude, owner_whole, prefe...  10.2 us
  transfers between devices with their start and end apart: 5, of which 5 were waited for; matrix products, arithmetic and copies ran while one was open for 2% of the time, Pallas kernels for 0%

profile of v1, /device:TPU:0, one launch (start us, length us, event | category | flops | bytes accessed | tf_op | source)
XLA Modules:
  0.0 444.8 jit_solution(14433480110356045769)
XLA Ops:
  6.5 8.8 %fusion.38 = (bf16[1,512,1,640]{3,2,1,0:T(2,128)(2,1)S(1)}, bf16[1,512,1,640]{3,2,1,0:T(2,128)(2,1)S(1)}, bf16[1,512,1,640]{3,2,1,0:T(2,128)(2,1)S(1)}, bf16[1,512,1,640]{3,2,1,0:T(2,128)(2,1)S(1)}) fusion(bf16[1,512,4,640]{3,2,1,0:T(4,128)(2,1)} %param.4), kind=kLoop, calls=%fused_computation.34 | loop fusion | bytes 5242880 | tf_op jit(solution)/shard_map/split | solution.py:16
  15.4 0.2 copy_bitcast_fusion.2
  15.6 0.2 copy_bitcast_fusion
  15.8 1.9 pad_maximum_fusion
  17.7 0.0 copy-start.2
  17.7 6.4 %all-to-all-start = ((bf16[4,1,512,1,640]{4,2,3,1,0:T(8,128)(2,1)}), bf16[4,1,512,1,640]{4,2,3,1,0:T(8,128)(2,1)S(1)}, u32[]{:S(2)}, u32[]{:S(2)}) async-start(bf16[4,1,512,1,640]{4,2,3,1,0:T(8,128)(2,1)} %pad_maximum_fusion), calls=%async_computation | async-start | bytes 5242880 | tf_op jit(solution)/shard_map/all_to_all | solution.py:16
  24.1 0.0 all-reduce.5.cloned.1.call-start
  24.1 0.0 copy-done.2
  24.1 0.6 fusion.40
  25.9 57.7 %all-to-all-done = bf16[4,1,512,1,640]{4,2,3,1,0:T(8,128)(2,1)S(1)} async-done(((bf16[4,1,512,1,640]{4,2,3,1,0:T(8,128)(2,1)}), bf16[4,1,512,1,640]{4,2,3,1,0:T(8,128)(2,1)S(1)}, u32[]{:S(2)}, u32[]{:S(2)}) %all-to-all-start) | async-done | bytes 2621472 | tf_op jit(solution)/shard_map/all_to_all | solution.py:16
  83.5 2.6 copy.18
  86.1 4.4 select_bitcast_fusion.1
  90.6 0.0 all-reduce.5.cloned.1.call-update
  90.6 0.0 all-gather.3.cloned.1.call-start
  90.7 188.5 %all-reduce.5.cloned.1.call-done = (bf16[4,512,1,640]{1,3,0,2:T(8,128)(2,1)}, bf16[4,512,1,640]{1,3,0,2:T(8,128)(2,1)}) async-done(((bf16[4,512,1,640]{1,3,0,2:T(8,128)(2,1)}, bf16[4,512,1,640]{1,3,0,2:T(8,128)(2,1)}), (bf16[4,512,1,640]{1,3,0,2:T(8,128)(2,1)}, bf16[4,512,1,640]{1,3,0,2:T(8,128)(2,1)})) %all-reduce.5.cloned.1.call-update) | async-done | bytes 5242896 | tf_op jit(solution)/shard_map/psum | solution.py:11
  279.1 0.0 all-gather.3.cloned.1.call-update
  279.2 0.0 all-gather.5.cloned.1.call-start
  279.2 0.7 all-gather.5.cloned.1.call-update
  279.9 0.2 all-reduce.7.cloned.1.call-start
  280.1 14.8 %all-gather.3.cloned.1.call-done = bf16[4,512,1,1280]{1,3,0,2:T(8,128)(2,1)} async-done(((bf16[4,512,1,640]{1,3,0,2:T(8,128)(2,1)}), bf16[4,512,1,1280]{1,3,0,2:T(8,128)(2,1)}) %all-gather.3.cloned.1.call-update) | async-done | bytes 5242896 | tf_op jit(solution)/shard_map/all_gather | solution.py:27
  294.9 7.9 %fusion.20 = bf16[1,1,640,1280]{2,3,0,1:T(8,128)(2,1)} fusion(bf16[4,512,1,1280]{1,3,0,2:T(8,128)(2,1)} %all-gather.3.cloned.1.call-done, bf16[4,1,512,1,640]{4,2,3,1,0:T(8,128)(2,1)S(1)} %all-to-all-done), kind=kOutput, calls=%fused_computation.15 | convolution fusion | flops 3356262400 | bytes 9502720 | tf_op jit(solution)/shard_map/sria,srjb->ijab/dot_general | solution.py:29
  302.8 10.1 %all-gather.5.cloned.1.call-done = bf16[4,512,1,1280]{1,3,0,2:T(8,128)(2,1)} async-done(((bf16[4,512,1,640]{1,3,0,2:T(8,128)(2,1)}), bf16[4,512,1,1280]{1,3,0,2:T(8,128)(2,1)}) %all-gather.5.cloned.1.call-update) | async-done | bytes 5242896 | tf_op jit(solution)/shard_map/all_gather | solution.py:27
  312.9 7.9 %fusion.23 = bf16[1,1,640,1280]{2,3,0,1:T(8,128)(2,1)} fusion(bf16[4,512,1,1280]{1,3,0,2:T(8,128)(2,1)} %all-gather.5.cloned.1.call-done, bf16[4,1,512,1,640]{4,2,3,1,0:T(8,128)(2,1)S(1)} %all-to-all-done), kind=kOutput, calls=%fused_computation.16 | convolution fusion | flops 3356262400 | bytes 9502720 | tf_op jit(solution)/shard_map/sria,srjb->ijab/dot_general | solution.py:29
  320.8 0.0 copy-start
  320.8 0.0 copy-start.1
  320.8 0.0 all-reduce.7.cloned.1.call-update
  324.4 0.0 copy-done
  324.4 0.7 fusion.39
  327.7 0.0 copy-done.1
  327.7 0.1 dynamic-slice_subtract_fusion.1
  327.8 83.1 %all-reduce.7.cloned.1.call-done = (bf16[1,1,640,1280]{2,3,0,1:T(8,128)(2,1)}, bf16[1,1,640,1280]{2,3,0,1:T(8,128)(2,1)}) async-done(((bf16[1,1,640,1280]{2,3,0,1:T(8,128)(2,1)}, bf16[1,1,640,1280]{2,3,0,1:T(8,128)(2,1)}), (bf16[1,1,640,1280]{2,3,0,1:T(8,128)(2,1)}, bf16[1,1,640,1280]{2,3,0,1:T(8,128)(2,1)})) %all-reduce.7.cloned.1.call-update) | async-done | bytes 3276816 | tf_op jit(solution)/shard_map/psum | solution.py:33
  410.9 0.0 copy-start.3
  410.9 7.6 %fusion = f32[4,512,640]{2,1,0:T(8,128)S(1)} fusion(bf16[4,512,1,1280]{1,3,0,2:T(8,128)(2,1)} %all-gather.5.cloned.1.call-done, bf16[1,1,640,1280]{2,3,0,1:T(8,128)(2,1)} %get-tuple-element.7, f32[640]{0:T(1024)S(1)} %get-tuple-element.16, f32[1280]{0:T(1024)S(1)} %copy-done.1), kind=kOutput, calls=%fused_computation | convolution fusion | flops 3358720000 | bytes 12131840 | tf_op jit(solution)/shard_map/ijab,srjb->sria/dot_general | solution.py:35
  418.6 0.0 copy-done.3
  418.6 9.4 %add_bitcast_fusion = f32[4,512,1,640]{3,1,0,2:T(8,128)} fusion(f32[4,512,640]{2,1,0:T(8,128)S(1)} %fusion, bf16[4,512,1,1280]{1,3,0,2:T(8,128)(2,1)} %all-gather.3.cloned.1.call-done, bf16[1,1,640,1280]{2,3,0,1:T(8,128)(2,1)S(1)} %copy-done.3, f32[1280]{0:T(1024)S(1)} %copy-done.1, f32[640]{0:T(1024)S(1)} %get-tuple-element.15), kind=kOutput, calls=%fused_computation.8 | convolution fusion | flops 3360030720 | bytes 17374720 | tf_op jit(solution)/shard_map/ijab,srjb->sria/dot_general | solution.py:35
  428.0 10.2 %copy.24 = f32[4,512,1,640]{3,2,1,0:T(1,128)} copy(f32[4,512,1,640]{3,1,0,2:T(8,128)} %add_bitcast_fusion) | data formatting | bytes 10485760 | tf_op jit(solution)/shard_map/add | solution.py:35
Async XLA Ops:
  17.7 6.5 %copy-start.2 = (s32[2]{0:T(128)S(1)}, s32[2]{0:T(128)}, u32[]{:S(2)}) copy-start(s32[2]{0:T(128)} %param.7) | copy-start | bytes 28
  17.7 65.9 %all-to-all-start = ((bf16[4,1,512,1,640]{4,2,3,1,0:T(8,128)(2,1)}), bf16[4,1,512,1,640]{4,2,3,1,0:T(8,128)(2,1)S(1)}, u32[]{:S(2)}, u32[]{:S(2)}) async-start(bf16[4,1,512,1,640]{4,2,3,1,0:T(8,128)(2,1)} %pad_maximum_fusion), calls=%async_computation | async-start | bytes 5242880 | tf_op jit(solution)/shard_map/all_to_all | solution.py:16
  24.1 255.0 %all-reduce.5.cloned.1.call-start = ((), (), s32[]{:S(2)}) async-start(), calls=%async_computation.3 | async-start | bytes 10485760 | tf_op jit(solution)/shard_map/psum | solution.py:11
  90.6 204.3 %all-gather.3.cloned.1.call-start = ((), (), s32[]{:S(2)}) async-start(), calls=%async_computation.1 | async-start | bytes 7864320 | tf_op jit(solution)/shard_map/all_gather | solution.py:27
  279.2 33.7 %all-gather.5.cloned.1.call-start = ((), (), s32[]{:S(2)}) async-start(), calls=%async_computation.2 | async-start | bytes 7864320 | tf_op jit(solution)/shard_map/all_gather | solution.py:27
  279.9 131.0 %all-reduce.7.cloned.1.call-start = ((), (), s32[]{:S(2)}) async-start(), calls=%async_computation.4 | async-start | bytes 6553600 | tf_op jit(solution)/shard_map/psum | solution.py:33
  320.8 3.6 copy-start
  320.8 6.9 %copy-start.1 = (f32[1280]{0:T(1024)S(1)}, f32[1280]{0:T(1024)}, u32[]{:S(2)}) copy-start(f32[1280]{0:T(1024)} %param.6) | copy-start | bytes 15364
  410.9 7.7 %copy-start.3 = (bf16[1,1,640,1280]{2,3,0,1:T(8,128)(2,1)S(1)}, bf16[1,1,640,1280]{2,3,0,1:T(8,128)(2,1)}, u32[]{:S(2)}) copy-start(bf16[1,1,640,1280]{2,3,0,1:T(8,128)(2,1)} %get-tuple-element.8) | copy-start | bytes 4915204
Sparse Core Ops, SparseCore 0:
  90.7 188.3 all-reduce.4
  280.7 14.1 all-gather.2
  296.5 16.3 all-gather.4
  320.9 89.9 all-reduce.6
